TPU v7x, 32 devices: a whole 2x2x4 slice. The times are simulated.
32 devices in a mesh: node: 2 (over y), gz: 16 (over z, x, core).
Axes of the slice: x: 2, y: 2, z: 4, core: 2. Of those that a mesh axis runs over, the one named last changes fastest.
Arguments:
- source: float32 [2, 64, 512, 256], P(None, ('node', 'gz')), parts along dimension 1, may hold values from -56 to 56
- layer_ids: int32 [64, 256], P(('node', 'gz')), parts along dimension 0, may hold values from 0 to 15
- conduct_table: float32 [16], replicated, may hold values from 0.35 to 3.75
- shift: float32 [4], P('node'), parts along dimension 0, may hold values from 0.2 to 1
Outputs:
- solution_field: float32 [2, 64, 512, 256], P(None, ('node', 'gz')), parts along dimension 1
- residual_norms: float32 [4], P('node'), parts along dimension 0
There are 2 independent parts, one for each index of `node`. A program takes and returns all parts, laid end to end along the dimension named above; an argument that names none is the same for every part. Nothing has to cross between parts.
All inputs are finite; a program needn't handle non-finite values.
Results may differ from a plain program's by a relative error of at most 0.0003.
Values sent between devices are 32-bit elements; how exact they have to be, the bound alone decides.
A program may use at most 64 MiB of HBM per device.

v0:
```python
import functools

import jax
import jax.numpy as jnp
import numpy as np
from jax import lax
from jax.experimental import pallas as pl
from jax.experimental.pallas import tpu as pltpu
from jax.sharding import PartitionSpec as P

ITERS = 2


relax = 0.6
highest = lax.Precision.HIGH


def with_halo(cells, sides, width):
    for axis, dim in sides:
        count = lax.axis_size(axis)
        ends = count - 1
        head = lax.slice_in_dim(cells, 0, width, axis=dim)
        tail = lax.slice_in_dim(cells, cells.shape[dim] - width, cells.shape[dim], axis=dim)
        cells = jnp.concatenate(
            [
                lax.ppermute(tail, axis, [(i, (i + 1) % count) for i in range(ends)]),
                cells,
                lax.ppermute(head, axis, [((i + 1) % count, i) for i in range(ends)]),
            ],
            axis=dim,
        )
    return cells


def sine_table(length):
    indices = lax.iota(jnp.int32, length) + 1
    product = indices[:, None] * indices[None, :] % (2 * (length + 1))
    return jnp.sqrt(2.0 / (length + 1)) * jnp.sin(
        jnp.pi / (length + 1) * product.astype(jnp.float32)
    )


def sine_eigen(length):
    indices = lax.iota(jnp.float32, length) + 1.0
    return 2.0 - 2.0 * jnp.cos(jnp.pi / (length + 1) * indices)


def dft_tables(length):
    indices = lax.iota(jnp.int32, length)
    product = indices[:, None] * indices[None, :] % length
    angles = 2.0 * jnp.pi / length * product.astype(jnp.float32)
    return (jnp.cos(angles), jnp.sin(angles))


def transform(field, cos_t, sin_t, inverse):

    def project(component, matrix):
        return jnp.einsum("zxy,xk->zky", component, matrix, precision=highest)

    re_cos = project(field[0], cos_t)
    re_sin = project(field[0], sin_t)
    im_cos = project(field[1], cos_t)
    im_sin = project(field[1], sin_t)
    if inverse:
        return jnp.stack([re_cos - im_sin, im_cos + re_sin]) / cos_t.shape[0]
    return jnp.stack([re_cos + im_sin, im_cos - re_sin])


def expand(weights):
    return weights[None, :, None, :]


def yz_part(field, upper, lower, conduct, cond_hi, cond_lo):
    cond_pad = jnp.pad(conduct, ((0, 0), (1, 1)), mode="edge")
    face_yp = 0.5 * (conduct + cond_pad[:, 2:])
    face_ym = 0.5 * (conduct + cond_pad[:, :-2])
    face_zp = 0.5 * (conduct + cond_hi)
    face_zm = 0.5 * (conduct + cond_lo)
    field_pad = jnp.pad(field, ((0, 0), (0, 0), (0, 0), (1, 1)))
    total = expand(face_yp) * (field - field_pad[..., 2:]) + expand(face_ym) * (
        field - field_pad[..., :-2]
    )
    return total + expand(face_zp) * (field - upper) + expand(face_zm) * (field - lower)


def shift_mult(shift_re, shift_im, field):
    return jnp.stack(
        [shift_re * field[0] - shift_im * field[1], shift_re * field[1] + shift_im * field[0]]
    )


def sine_both(field, sine_y, sine_z):
    field = jnp.einsum("pzxy,yj->pzxj", field, sine_y, precision=highest)
    return jnp.einsum("pzxy,zk->pkxy", field, sine_z, precision=highest)


def precondition(coeffs, mode_eig, mean_cond, shift_re, shift_im, sine_y, sine_z, eig_y, eig_z):
    coeffs = sine_both(coeffs, sine_y, sine_z)
    eigen = eig_z[:, None, None] + mode_eig[None, :, None] + eig_y[None, None, :]
    real_den = shift_re + mean_cond * eigen
    inv = 1.0 / (real_den * real_den + shift_im * shift_im)
    scaled = jnp.stack(
        [
            (coeffs[0] * real_den + coeffs[1] * shift_im) * inv,
            (coeffs[1] * real_den - coeffs[0] * shift_im) * inv,
        ]
    )
    return sine_both(scaled, sine_y, sine_z)


def body_plain(source, layer_ids, conduct_table, shift):
    shift_re = shift[0]
    shift_im = shift[1]
    planes = source.shape[1]
    length_x = source.shape[2]
    length_y = source.shape[3]
    groups = lax.axis_size("gz")
    length_z = planes * groups
    modes = length_x // groups
    first_mode = lax.axis_index("gz") * modes
    layers = conduct_table.shape[0]
    onehot = layer_ids[:, :, None] == lax.iota(jnp.int32, layers)[None, None, :]
    local = jnp.sum(jnp.where(onehot, conduct_table[None, None, :], 0.0), axis=-1)
    conduct = lax.all_gather(local, "gz", axis=0, tiled=True)
    mean_cond = jnp.sum(conduct) / (length_y * length_z)
    cond_z = jnp.pad(conduct, ((1, 1), (0, 0)), mode="edge")
    cos_t, sin_t = dft_tables(length_x)
    sine_y = sine_table(length_y)
    sine_z = sine_table(length_z)
    eig_y = sine_eigen(length_y)
    eig_z = sine_eigen(length_z)
    mode_ids = (first_mode + lax.iota(jnp.int32, modes)).astype(jnp.float32)
    mode_eig = 2.0 - 2.0 * jnp.cos(2.0 * jnp.pi / length_x * mode_ids)
    cells = length_x * length_y * length_z
    spectra = transform(source, cos_t, sin_t, False)
    forcing = lax.all_to_all(spectra, "gz", split_axis=2, concat_axis=1, tiled=True)
    partials = []
    solution = jnp.zeros_like(forcing)
    for iteration in range(ITERS):
        if iteration == 0:
            resid = forcing
        else:
            padded = jnp.pad(solution, ((0, 0), (1, 1), (0, 0), (0, 0)))
            lap = expand(conduct) * mode_eig[None, None, :, None] * solution
            lap = lap + yz_part(
                solution, padded[:, 2:], padded[:, :-2], conduct, cond_z[2:], cond_z[:-2]
            )
            resid = forcing - (shift_mult(shift_re, shift_im, solution) + lap)
        partials.append(jnp.sum(resid * resid) / length_x)
        update = precondition(
            resid, mode_eig, mean_cond, shift_re, shift_im, sine_y, sine_z, eig_y, eig_z
        )
        solution = solution + relax * update
    slabs = lax.all_to_all(solution, "gz", split_axis=1, concat_axis=2, tiled=True)
    result = transform(slabs, cos_t, sin_t, True)
    sums = jnp.sum(lax.all_gather(jnp.stack(partials)[None, :], "gz", axis=0, tiled=True), axis=0)
    return (result, jnp.sqrt(sums / cells))


RADIX = 4


def halves(table):
    high = table.astype(jnp.bfloat16)
    low = (table - high.astype(np.float32)).astype(jnp.bfloat16)
    return (jnp.asarray(high), jnp.asarray(low))


def radix_tables(length_x):
    count = length_x // RADIX
    pos = np.arange(count)
    forward = []
    for residue in range(RADIX):
        modes = RADIX * pos + residue
        angle = 2.0 * np.pi / length_x * (modes[:, None] * pos[None, :] % length_x)
        cos_t, sin_t = np.cos(angle), np.sin(angle)
        forward.append(np.block([[cos_t, sin_t], [-sin_t, cos_t]]))
    forward = np.stack(forward)
    backward = np.swapaxes(forward, 1, 2) / length_x
    return (forward.astype(np.float32), backward.astype(np.float32))


def sine_host(length):
    indices = np.arange(length) + 1
    product = indices[:, None] * indices[None, :] % (2 * (length + 1))
    return (np.sqrt(2.0 / (length + 1)) * np.sin(np.pi / (length + 1) * product)).astype(np.float32)


def split(values):
    high = values.astype(jnp.bfloat16)
    return (high, (values - high.astype(jnp.float32)).astype(jnp.bfloat16))


def dot3(left, right):
    mul = functools.partial(jnp.dot, preferred_element_type=jnp.float32)
    return mul(left[0], right[0]) + (mul(left[0], right[1]) + mul(left[1], right[0]))


def turn(re, im, quarter):
    quarter = quarter % 4
    return [(re, im), (-im, re), (-re, -im), (im, -re)][quarter]


def combine(parts, quarters):
    re, im = turn(*parts[0], quarters[0])
    for part, quarter in zip(parts[1:], quarters[1:]):
        more_re, more_im = turn(*part, quarter)
        re, im = re + more_re, im + more_im
    return (re, im)


def kernel(
    groups,
    planes,
    source,
    conduct,
    mode_eig,
    base,
    shift,
    fwd_hi,
    fwd_lo,
    bwd_hi,
    bwd_lo,
    sine_hi,
    sine_lo,
    out,
    norms,
    spectra,
    forcing,
    cond_all,
    cond,
    work,
    alpha,
    field,
    slabs,
    sums,
    in_send,
    in_recv,
    cond_send,
    cond_recv,
    out_send,
    out_recv,
    sum_send,
    sum_recv,
):
    me = lax.axis_index("gz")
    length_x = source.shape[2]
    length_y = source.shape[3]
    length_z = groups * planes
    count = length_x // RADIX
    modes = length_x // groups
    owners = groups // RADIX
    step = min(8, length_z)

    def peer(offset):
        return lax.rem(me + offset, groups)

    def back(offset):
        return lax.rem(me + groups - offset, groups)

    def remote(src, dst, send, recv, target):
        return pltpu.make_async_remote_copy(
            src_ref=src,
            dst_ref=dst,
            send_sem=send,
            recv_sem=recv,
            device_id={"gz": target},
            device_id_type=pl.DeviceIdType.MESH,
        )

    def rows(index):
        return pl.ds(index * planes, planes)

    def cond_copy(offset):
        return remote(
            conduct, cond_all.at[me], cond_send.at[offset], cond_recv.at[offset], peer(offset)
        )

    def in_copy(target, offset):
        return remote(
            spectra.at[target], forcing.at[rows(me)], in_send.at[offset], in_recv.at[offset], target
        )

    def out_copy(target, offset):
        return remote(
            work.at[rows(target)], slabs.at[me], out_send.at[offset], out_recv.at[offset], target
        )

    def sum_copy(offset):
        return remote(
            sums.at[me], sums.at[me], sum_send.at[offset], sum_recv.at[offset], peer(offset)
        )

    def each_peer(act):
        def run(offset, carry):
            act(offset)
            return carry

        lax.fori_loop(1, groups, run, 0)

    barrier = pltpu.get_barrier_semaphore()

    @each_peer
    def _(offset):
        pl.semaphore_signal(
            barrier, inc=1, device_id={"gz": peer(offset)}, device_id_type=pl.DeviceIdType.MESH
        )

    pl.semaphore_wait(barrier, groups - 1)

    @each_peer
    def _(offset):
        cond_copy(offset).start()

    cond_all[me] = conduct[...]

    for residue in range(RADIX):

        def forward(plane, carry):
            parts = [
                (
                    source[0, plane, q * count : (q + 1) * count, :],
                    source[1, plane, q * count : (q + 1) * count, :],
                )
                for q in range(RADIX)
            ]
            mixed = combine(parts, [-residue * q for q in range(RADIX)])
            right = split(jnp.concatenate(mixed, axis=0))
            result = dot3((fwd_hi[residue], fwd_lo[residue]), right)
            for owner in range(owners):
                for part in range(2):
                    start = part * count + owner * modes
                    spectra[residue * owners + owner, plane, part] = result[start : start + modes]
            return carry

        lax.fori_loop(0, planes, forward, 0)
        for owner in range(owners):
            target = residue * owners + owner
            offset = lax.rem(target + groups - me, groups)

            @pl.when(target != me)
            def _():
                in_copy(target, offset).start()

    forcing[rows(me)] = spectra[me]

    @each_peer
    def _(offset):
        cond_copy(offset).wait()

    def spread(index, total):
        for plane in range(planes):
            row = jnp.broadcast_to(cond_all[index, plane : plane + 1, :], (8, length_y))
            cond[index * planes + plane + 1] = row
            total = total + row
        return total

    total = lax.fori_loop(0, groups, spread, jnp.zeros((8, length_y), jnp.float32))
    cond[0] = cond[1]
    cond[length_z + 1] = cond[length_z]
    mean_cond = jnp.sum(total) / (8 * length_y * length_z)
    shift_re = shift[0]
    shift_im = shift[1]
    scale = relax / mean_cond
    diag_re = base[...] + shift_re / mean_cond
    diag_im = shift_im / mean_cond
    none = jnp.zeros((modes, length_y), jnp.float32)

    def factor(level, carry):
        gap_re = diag_re - carry[0]
        gap_im = diag_im - carry[1]
        inverse = 1.0 / (gap_re * gap_re + gap_im * gap_im)
        now = (gap_re * inverse, -gap_im * inverse)
        alpha[level, 0] = now[0]
        alpha[level, 1] = now[1]
        return now

    lax.fori_loop(0, length_z, factor, (none, none))

    @each_peer
    def _(offset):
        in_copy(peer(offset), offset).wait()

    sine = (sine_hi[...], sine_lo[...])

    def sine_rows(read, write):
        def run(index, carry):
            first = index * step
            values = read(first).reshape(step * 2 * modes, length_y)
            result = dot3(split(values), sine)
            write(first, result.reshape(step, 2, modes, length_y))
            return carry

        lax.fori_loop(0, length_z // step, run, 0)

    def put_work(first, values):
        work[pl.ds(first, step)] = values

    def sweep():
        def down(level, carry):
            re = work[level, 0] + carry[0]
            im = work[level, 1] + carry[1]
            a_re = alpha[level, 0]
            a_im = alpha[level, 1]
            now = (a_re * re - a_im * im, a_re * im + a_im * re)
            work[level, 0] = now[0]
            work[level, 1] = now[1]
            return now

        def up(count_up, carry):
            level = length_z - 1 - count_up
            a_re = alpha[level, 0]
            a_im = alpha[level, 1]
            now = (
                work[level, 0] + (a_re * carry[0] - a_im * carry[1]),
                work[level, 1] + (a_re * carry[1] + a_im * carry[0]),
            )
            work[level, 0] = now[0]
            work[level, 1] = now[1]
            return now

        lax.fori_loop(0, length_z, down, (none, none))
        lax.fori_loop(0, length_z, up, (none, none))

    def put_field(first, values):
        field[pl.ds(first + 1, step)] = values * scale

    lane = lax.broadcasted_iota(jnp.int32, (modes, length_y), 1)
    row_lane = lax.broadcasted_iota(jnp.int32, (8, length_y), 1)
    last = length_y - 1

    def residual(level, carry):
        here = cond[level + 1]
        right = jnp.where(row_lane == last, here, pltpu.roll(here, last, 1))
        left = jnp.where(row_lane == 0, here, pltpu.roll(here, 1, 1))
        face_yp = (0.5 * (here + right))[0:1]
        face_ym = (0.5 * (here + left))[0:1]
        face_zp = (0.5 * (here + cond[level + 2]))[0:1]
        face_zm = (0.5 * (here + cond[level]))[0:1]
        center = here[0:1] * mode_eig[...] + (face_yp + face_ym + face_zp + face_zm) + shift_re
        values = [field[level + 1, part] for part in range(2)]
        turned = [-shift_im * values[1], shift_im * values[0]]
        squares = list(carry)
        for part in range(2):
            value = values[part]
            right = jnp.where(lane == last, 0.0, pltpu.roll(value, last, 1))
            left = jnp.where(lane == 0, 0.0, pltpu.roll(value, 1, 1))
            applied = center * value + turned[part]
            applied = applied - face_yp * right - face_ym * left
            applied = applied - face_zp * field[level + 2, part] - face_zm * field[level, part]
            given = forcing[level, part]
            rest = given - applied
            work[level, part] = rest
            squares[0] = squares[0] + given * given
            squares[1] = squares[1] + rest * rest
        return tuple(squares)

    for part in range(2):
        field[0, part] = none
        field[length_z + 1, part] = none
    sine_rows(lambda first: forcing[pl.ds(first, step)], put_work)
    sweep()
    sine_rows(lambda first: work[pl.ds(first, step)], put_field)
    squares = lax.fori_loop(0, length_z, residual, (none, none))
    row = lax.broadcasted_iota(jnp.int32, (8, 128), 0)
    sums[me] = jnp.where(row == 0, jnp.sum(squares[0]), jnp.sum(squares[1])) / length_x

    @each_peer
    def _(offset):
        sum_copy(offset).start()

    sine_rows(lambda first: work[pl.ds(first, step)], put_work)
    sweep()

    def finish_rows(index, carry):
        first = index * step
        values = work[pl.ds(first, step)].reshape(step * 2 * modes, length_y)
        result = dot3(split(values), sine).reshape(step, 2, modes, length_y)
        work[pl.ds(first, step)] = field[pl.ds(first + 1, step)] + scale * result
        for block in range(step // planes):
            target = index * (step // planes) + block
            offset = lax.rem(target + groups - me, groups)

            @pl.when(target != me)
            def _():
                out_copy(target, offset).start()

        return carry

    lax.fori_loop(0, length_z // step, finish_rows, 0)
    slabs[me] = work[rows(me)]

    @each_peer
    def _(offset):
        sum_copy(offset).wait()

    norms[...] = jnp.sum(sums[...], axis=0)

    @each_peer
    def _(offset):
        out_copy(peer(offset), offset).wait()

    def inverse(plane, carry):
        parts = []
        for residue in range(RADIX):
            blocks = [
                slabs[residue * owners + owner, plane, part]
                for part in range(2)
                for owner in range(owners)
            ]
            right = split(jnp.concatenate(blocks, axis=0))
            result = dot3((bwd_hi[residue], bwd_lo[residue]), right)
            parts.append((result[:count], result[count:]))
        for q in range(RADIX):
            re, im = combine(parts, [residue * q for residue in range(RADIX)])
            out[0, plane, q * count : (q + 1) * count, :] = re
            out[1, plane, q * count : (q + 1) * count, :] = im
        return carry

    lax.fori_loop(0, planes, inverse, 0)


def body(source, layer_ids, conduct_table, shift):
    planes = source.shape[1]
    length_x = source.shape[2]
    length_y = source.shape[3]
    groups = lax.axis_size("gz")
    length_z = planes * groups
    modes = length_x // groups
    if groups % RADIX or modes % 8 or length_z % 8 or 8 % planes:
        return body_plain(source, layer_ids, conduct_table, shift)
    me = lax.axis_index("gz")
    owners = groups // RADIX
    layers = conduct_table.shape[0]
    onehot = layer_ids[:, :, None] == lax.iota(jnp.int32, layers)[None, None, :]
    conduct = jnp.sum(jnp.where(onehot, conduct_table[None, None, :], 0.0), axis=-1)
    conduct = jnp.pad(conduct, ((0, 8 - planes), (0, 0)))
    mode_ids = RADIX * (me % owners * modes + lax.iota(jnp.int32, modes)) + me // owners
    mode_eig = 2.0 - 2.0 * jnp.cos(2.0 * jnp.pi / length_x * mode_ids.astype(jnp.float32))
    mode_eig = jnp.broadcast_to(mode_eig[:, None], (modes, length_y))
    base = mode_eig + (sine_eigen(length_y) + 2.0)[None, :]
    forward, backward = radix_tables(length_x)
    tables = [*halves(forward), *halves(backward), *halves(sine_host(length_y))]
    block = (length_z, 2, modes, length_y)
    vmem = pl.BlockSpec(memory_space=pltpu.VMEM)
    result, norms = pl.pallas_call(
        functools.partial(kernel, groups, planes),
        out_shape=(
            jax.ShapeDtypeStruct(source.shape, jnp.float32),
            jax.ShapeDtypeStruct((8, 128), jnp.float32),
        ),
        in_specs=[vmem] * 4 + [pl.BlockSpec(memory_space=pltpu.SMEM)] + [vmem] * 6,
        out_specs=(vmem, vmem),
        scratch_shapes=[
            pltpu.VMEM((groups, planes, 2, modes, length_y), jnp.float32),
            pltpu.VMEM(block, jnp.float32),
            pltpu.VMEM((groups, 8, length_y), jnp.float32),
            pltpu.VMEM((length_z + 2, 8, length_y), jnp.float32),
            pltpu.VMEM(block, jnp.float32),
            pltpu.VMEM(block, jnp.float32),
            pltpu.VMEM((length_z + 2, 2, modes, length_y), jnp.float32),
            pltpu.VMEM((groups, planes, 2, modes, length_y), jnp.float32),
            pltpu.VMEM((groups, 8, 128), jnp.float32),
        ]
        + [pltpu.SemaphoreType.DMA((groups,))] * 8,
        compiler_params=pltpu.CompilerParams(
            collective_id=0, has_side_effects=True, vmem_limit_bytes=48 << 20
        ),
    )(source, conduct, mode_eig, base, shift, *tables)
    cells = length_x * length_y * length_z
    return (result, jnp.sqrt(norms[:ITERS, 0] / cells))


def solution(mesh):
    placed = (P(None, ("node", "gz"), None, None), P(("node", "gz"), None), P(), P("node"))
    return jax.shard_map(
        body,
        mesh=mesh,
        in_specs=placed,
        out_specs=(P(None, ("node", "gz"), None, None), P("node")),
        check_vma=False,
    )
```

profile of v0, /device:TPU:27, one launch (start us, length us, event | category | flops | bytes accessed | tf_op | source)
XLA Modules:
  0.0 126.4 jit_solution(11149431845207278220)
XLA Ops:
  0.8 0.8 select_reduce_fusion
  1.5 0.1 broadcast_add_fusion.base
  1.6 0.1 broadcast_in_dim.24.mode_eig
  1.7 0.0 copy-start
  1.7 1.0 copy-done
  2.7 0.0 copy-start.1
  2.7 1.0 copy-done.1
  3.8 0.0 copy-start.2
  3.8 1.0 copy-done.2
  4.8 0.0 copy-start.3
  4.8 1.0 copy-done.3
  5.9 0.0 copy-start.4
  5.9 0.9 copy-done.4
  6.8 0.0 copy-start.5
  6.8 0.9 copy-done.5
  7.7 0.0 copy-start.6
  7.7 0.7 copy-done.6
  8.3 116.1 %shard_map.113 = (f32[2,2,512,256]{3,2,1,0:T(8,128)S(1)}, f32[8,128]{1,0:T(8,128)S(1)}) custom-call(f32[2,2,512,256]{3,2,1,0:T(8,128)} %source.1, f32[8,256]{1,0:T(8,128)S(1)} %pad.4.conduct, f32[32,256]{1,0:T(8,128)S(1)} %broadcast_in_dim.24.mode_eig, f32[32,256]{1,0:T(8,128)S(1)} %broadcast_add_fusion.base, f32[2]{0:T(128)S(1)} %copy-done.6, ...), custom_call_target="tpu_custom_call" | custom-call | tf_op jit(solution)/shard_map/pallas_call | solution.py:546
  124.4 0.6 sqrt_reduce_fusion
  125.1 1.3 %copy.13 = f32[2,2,512,256]{3,2,1,0:T(8,128)} copy(f32[2,2,512,256]{3,2,1,0:T(8,128)S(1)} %get-tuple-element.8) | data formatting | bytes 4194304
  (3 shorter events, 0.1 us)
Async XLA Ops:
  1.7 1.0 copy-start
  2.7 1.0 copy-start.1
  3.8 1.0 copy-start.2
  4.8 1.0 copy-start.3
  5.9 0.9 copy-start.4
  6.8 0.9 copy-start.5
  7.7 0.7 copy-start.6
where the time goes:
time: 127 us; the launch traced here: 126 us
  Pallas kernels  116 us (91%)
  local copies, waits for them, and re-layouts  8.03 us (6%)
  other arithmetic  1.59 us (1%)
    pallas_call x1, Pallas kernels, body(): pl.pallas_call(functools.partial(kernel, groups, planes), out_shape=(jax....  116 us
    unnamed x15, local copies, waits for them, and re-layouts  7.95 us

commit v1 on v0

--- a/solution.py
+++ b/solution.py
@@ -209,31 +209,55 @@
     return (re, im)
 
 
+def times(left, right):
+    return (left[0] * right[0] - left[1] * right[1], left[0] * right[1] + left[1] * right[0])
+
+
+def plus(left, right):
+    return (left[0] + right[0], left[1] + right[1])
+
+
 def kernel(
     groups,
     planes,
-    source,
+    chunks,
+    source_hbm,
     conduct,
     mode_eig,
     base,
     shift,
+    fwd_hi_hbm,
+    fwd_lo_hbm,
+    bwd_hi_hbm,
+    bwd_lo_hbm,
+    sine_hi_hbm,
+    sine_lo_hbm,
+    out,
+    norms,
+    source,
     fwd_hi,
     fwd_lo,
     bwd_hi,
     bwd_lo,
     sine_hi,
     sine_lo,
-    out,
-    norms,
     spectra,
     forcing,
     cond_all,
     cond,
     work,
     alpha,
+    lines,
     field,
+    result,
     slabs,
     sums,
+    squares,
+    up_out,
+    up_in,
+    down_out,
+    down_in,
+    load_sem,
     in_send,
     in_recv,
     cond_send,
@@ -242,21 +266,40 @@
     out_recv,
     sum_send,
     sum_recv,
+    up_send,
+    up_recv,
+    down_send,
+    down_recv,
 ):
     me = lax.axis_index("gz")
+    side = lax.rem(me, RADIX)
+    team = me // RADIX
+    teams = groups // RADIX
     length_x = source.shape[2]
     length_y = source.shape[3]
     length_z = groups * planes
+    depth = RADIX * planes
     count = length_x // RADIX
-    modes = length_x // groups
-    owners = groups // RADIX
-    step = min(8, length_z)
-
-    def peer(offset):
-        return lax.rem(me + offset, groups)
-
-    def back(offset):
-        return lax.rem(me + groups - offset, groups)
+    modes = count // chunks
+    first_level = team * depth
+    last_level = length_z - first_level - depth
+
+    loads = [
+        pltpu.make_async_copy(src, dst, load_sem.at[index])
+        for index, (src, dst) in enumerate(
+            [
+                (source_hbm, source),
+                (fwd_hi_hbm, fwd_hi),
+                (fwd_lo_hbm, fwd_lo),
+                (sine_hi_hbm, sine_hi),
+                (sine_lo_hbm, sine_lo),
+                (bwd_hi_hbm, bwd_hi),
+                (bwd_lo_hbm, bwd_lo),
+            ]
+        )
+    ]
+    for load in loads:
+        load.start()
 
     def remote(src, dst, send, recv, target):
         return pltpu.make_async_remote_copy(
@@ -268,6 +311,12 @@
             device_id_type=pl.DeviceIdType.MESH,
         )
 
+    def peer(offset):
+        return lax.rem(me + offset, groups)
+
+    def mate(offset):
+        return lax.rem(side + offset, RADIX)
+
     def rows(index):
         return pl.ds(index * planes, planes)
 
@@ -276,19 +325,47 @@
             conduct, cond_all.at[me], cond_send.at[offset], cond_recv.at[offset], peer(offset)
         )
 
-    def in_copy(target, offset):
-        return remote(
-            spectra.at[target], forcing.at[rows(me)], in_send.at[offset], in_recv.at[offset], target
-        )
-
-    def out_copy(target, offset):
-        return remote(
-            work.at[rows(target)], slabs.at[me], out_send.at[offset], out_recv.at[offset], target
-        )
-
     def sum_copy(offset):
         return remote(
             sums.at[me], sums.at[me], sum_send.at[offset], sum_recv.at[offset], peer(offset)
+        )
+
+    def in_copy(chunk, offset):
+        target = mate(offset)
+        return remote(
+            spectra.at[target, chunk],
+            forcing.at[chunk, rows(side)],
+            in_send.at[chunk, offset],
+            in_recv.at[chunk, offset],
+            team * RADIX + target,
+        )
+
+    def out_copy(chunk, offset):
+        target = mate(offset)
+        return remote(
+            result.at[chunk, rows(target)],
+            slabs.at[side, chunk],
+            out_send.at[chunk, offset],
+            out_recv.at[chunk, offset],
+            team * RADIX + target,
+        )
+
+    def up_copy(turn_id, chunk):
+        return remote(
+            up_out.at[turn_id, chunk],
+            up_in.at[turn_id, chunk],
+            up_send.at[turn_id, chunk],
+            up_recv.at[turn_id, chunk],
+            lax.rem(me + RADIX, groups),
+        )
+
+    def down_copy(turn_id, chunk):
+        return remote(
+            down_out.at[turn_id, chunk],
+            down_in.at[turn_id, chunk],
+            down_send.at[turn_id, chunk],
+            down_recv.at[turn_id, chunk],
+            lax.rem(me + groups - RADIX, groups),
         )
 
     def each_peer(act):
@@ -298,6 +375,13 @@
 
         lax.fori_loop(1, groups, run, 0)
 
+    def pair(ref, *index):
+        return (ref[(*index, 0)], ref[(*index, 1)])
+
+    def put(ref, values, *index):
+        ref[(*index, 0)] = values[0]
+        ref[(*index, 1)] = values[1]
+
     barrier = pltpu.get_barrier_semaphore()
 
     @each_peer
@@ -313,36 +397,39 @@
         cond_copy(offset).start()
 
     cond_all[me] = conduct[...]
-
-    for residue in range(RADIX):
-
-        def forward(plane, carry):
-            parts = [
-                (
-                    source[0, plane, q * count : (q + 1) * count, :],
-                    source[1, plane, q * count : (q + 1) * count, :],
-                )
-                for q in range(RADIX)
-            ]
+    for load in loads[:3]:
+        load.wait()
+
+    def forward(plane, carry):
+        parts = [
+            (
+                source[0, plane, q * count : (q + 1) * count, :],
+                source[1, plane, q * count : (q + 1) * count, :],
+            )
+            for q in range(RADIX)
+        ]
+        for residue in range(RADIX):
             mixed = combine(parts, [-residue * q for q in range(RADIX)])
             right = split(jnp.concatenate(mixed, axis=0))
-            result = dot3((fwd_hi[residue], fwd_lo[residue]), right)
-            for owner in range(owners):
+            values = dot3((fwd_hi[residue], fwd_lo[residue]), right)
+            for chunk in range(chunks):
                 for part in range(2):
-                    start = part * count + owner * modes
-                    spectra[residue * owners + owner, plane, part] = result[start : start + modes]
-            return carry
-
-        lax.fori_loop(0, planes, forward, 0)
-        for owner in range(owners):
-            target = residue * owners + owner
-            offset = lax.rem(target + groups - me, groups)
-
-            @pl.when(target != me)
-            def _():
-                in_copy(target, offset).start()
-
-    forcing[rows(me)] = spectra[me]
+                    start = part * count + chunk * modes
+                    spectra[residue, chunk, plane, part] = values[start : start + modes]
+        return carry
+
+    lax.fori_loop(0, planes, forward, 0)
+    for chunk in range(chunks):
+        for offset in (2, 3, 1):
+            in_copy(chunk, offset).start()
+
+    def keep(chunk, carry):
+        forcing[chunk, rows(side)] = spectra[side, chunk]
+        return carry
+
+    lax.fori_loop(0, chunks, keep, 0)
+    for load in loads[3:]:
+        load.wait()
 
     @each_peer
     def _(offset):
@@ -362,106 +449,195 @@
     shift_re = shift[0]
     shift_im = shift[1]
     scale = relax / mean_cond
-    diag_re = base[...] + shift_re / mean_cond
+    offset_re = shift_re / mean_cond
     diag_im = shift_im / mean_cond
     none = jnp.zeros((modes, length_y), jnp.float32)
-
-    def factor(level, carry):
-        gap_re = diag_re - carry[0]
-        gap_im = diag_im - carry[1]
-        inverse = 1.0 / (gap_re * gap_re + gap_im * gap_im)
-        now = (gap_re * inverse, -gap_im * inverse)
-        alpha[level, 0] = now[0]
-        alpha[level, 1] = now[1]
-        return now
-
-    lax.fori_loop(0, length_z, factor, (none, none))
-
-    @each_peer
-    def _(offset):
-        in_copy(peer(offset), offset).wait()
+    one = jnp.ones((modes, length_y), jnp.float32)
+
+    def factors(chunk):
+        diag_re = base[chunk] + offset_re
+
+        def factor(level, carry):
+            gap_re = diag_re - carry[0]
+            gap_im = diag_im - carry[1]
+            inverse = 1.0 / (gap_re * gap_re + gap_im * gap_im)
+            now = (gap_re * inverse, -gap_im * inverse)
+            put(alpha, now, chunk, level)
+            return now
+
+        put(alpha, (none, none), chunk, 0)
+        lax.fori_loop(1, length_z + 1, factor, (none, none))
 
     sine = (sine_hi[...], sine_lo[...])
 
-    def sine_rows(read, write):
+    def sine_rows(values):
+        flat = values.reshape(values.shape[0] * 2 * modes, length_y)
+        return dot3(split(flat), sine).reshape(values.shape)
+
+    def partial_up(chunk):
         def run(index, carry):
-            first = index * step
-            values = read(first).reshape(step * 2 * modes, length_y)
-            result = dot3(split(values), sine)
-            write(first, result.reshape(step, 2, modes, length_y))
-            return carry
-
-        lax.fori_loop(0, length_z // step, run, 0)
-
-    def put_work(first, values):
-        work[pl.ds(first, step)] = values
-
-    def sweep():
-        def down(level, carry):
-            re = work[level, 0] + carry[0]
-            im = work[level, 1] + carry[1]
-            a_re = alpha[level, 0]
-            a_im = alpha[level, 1]
-            now = (a_re * re - a_im * im, a_re * im + a_im * re)
-            work[level, 0] = now[0]
-            work[level, 1] = now[1]
+            factor = pair(alpha, chunk, first_level + index + 1)
+            value = times(factor, plus(pair(work, chunk, index), carry[:2]))
+            return (*value, *times(factor, carry[2:]))
+
+        return lax.fori_loop(0, depth, run, (none, none, one, none))
+
+    def partial_down(chunk):
+        def run(index, carry):
+            factor = pair(alpha, chunk, last_level + index + 1)
+            value = times(factor, plus(pair(work, chunk, depth - 1 - index), carry[:2]))
+            return (*value, *times(factor, carry[2:]))
+
+        return lax.fori_loop(0, depth, run, (none, none, one, none))
+
+    def launch(turn_id, chunk):
+        rise = partial_up(chunk)
+        put(up_out, rise[:2], turn_id, chunk)
+
+        @pl.when(team == 0)
+        def _():
+            put(up_in, (none, none), turn_id, chunk)
+            up_copy(turn_id, chunk).start()
+
+        fall = partial_down(chunk)
+        put(down_out, fall[:2], turn_id, chunk)
+
+        @pl.when(team == teams - 1)
+        def _():
+            put(down_in, (none, none), turn_id, chunk)
+            down_copy(turn_id, chunk).start()
+
+        put(lines, rise[2:], chunk, 0)
+        put(lines, fall[2:], chunk, 1)
+
+    def relay(turn_id, chunk):
+        @pl.when(team > 0)
+        def _():
+            up_copy(turn_id, chunk).wait_recv()
+
+            @pl.when(team < teams - 1)
+            def _():
+                more = times(pair(lines, chunk, 0), pair(up_in, turn_id, chunk))
+                put(up_out, plus(pair(up_out, turn_id, chunk), more), turn_id, chunk)
+                up_copy(turn_id, chunk).start()
+
+        @pl.when(team < teams - 1)
+        def _():
+            down_copy(turn_id, chunk).wait_recv()
+
+            @pl.when(team > 0)
+            def _():
+                more = times(pair(lines, chunk, 1), pair(down_in, turn_id, chunk))
+                put(down_out, plus(pair(down_out, turn_id, chunk), more), turn_id, chunk)
+                down_copy(turn_id, chunk).start()
+
+    def solve(turn_id, chunk):
+        below = pair(up_in, turn_id, chunk)
+        above = pair(down_in, turn_id, chunk)
+
+        def ahead(index, carry):
+            factor = pair(alpha, chunk, first_level + index + 1)
+            now = times(factor, plus(pair(work, chunk, index), carry))
+            put(work, now, chunk, index)
             return now
 
-        def up(count_up, carry):
-            level = length_z - 1 - count_up
-            a_re = alpha[level, 0]
-            a_im = alpha[level, 1]
-            now = (
-                work[level, 0] + (a_re * carry[0] - a_im * carry[1]),
-                work[level, 1] + (a_re * carry[1] + a_im * carry[0]),
-            )
-            work[level, 0] = now[0]
-            work[level, 1] = now[1]
+        reached = lax.fori_loop(0, depth, ahead, below)
+        factor = pair(alpha, chunk, first_level + depth)
+        edge = pair(alpha, chunk, last_level)
+        loop = times(factor, edge)
+        gap_re = 1.0 - loop[0]
+        inverse = 1.0 / (gap_re * gap_re + loop[1] * loop[1])
+        top = plus(reached, times(factor, above))
+        top = times(top, (gap_re * inverse, loop[1] * inverse))
+        outer = plus(above, times(edge, top))
+        put(work, outer, chunk, depth + 1)
+
+        def behind(step, carry):
+            index = depth - 1 - step
+            factor = pair(alpha, chunk, first_level + index + 1)
+            now = plus(pair(work, chunk, index), times(factor, carry))
+            put(work, now, chunk, index)
             return now
 
-        lax.fori_loop(0, length_z, down, (none, none))
-        lax.fori_loop(0, length_z, up, (none, none))
-
-    def put_field(first, values):
-        field[pl.ds(first + 1, step)] = values * scale
+        bottom = lax.fori_loop(0, depth, behind, outer)
+        put(work, plus(below, times(pair(alpha, chunk, first_level), bottom)), chunk, depth)
 
     lane = lax.broadcasted_iota(jnp.int32, (modes, length_y), 1)
     row_lane = lax.broadcasted_iota(jnp.int32, (8, length_y), 1)
     last = length_y - 1
 
-    def residual(level, carry):
-        here = cond[level + 1]
-        right = jnp.where(row_lane == last, here, pltpu.roll(here, last, 1))
-        left = jnp.where(row_lane == 0, here, pltpu.roll(here, 1, 1))
-        face_yp = (0.5 * (here + right))[0:1]
-        face_ym = (0.5 * (here + left))[0:1]
-        face_zp = (0.5 * (here + cond[level + 2]))[0:1]
-        face_zm = (0.5 * (here + cond[level]))[0:1]
-        center = here[0:1] * mode_eig[...] + (face_yp + face_ym + face_zp + face_zm) + shift_re
-        values = [field[level + 1, part] for part in range(2)]
-        turned = [-shift_im * values[1], shift_im * values[0]]
-        squares = list(carry)
-        for part in range(2):
-            value = values[part]
-            right = jnp.where(lane == last, 0.0, pltpu.roll(value, last, 1))
-            left = jnp.where(lane == 0, 0.0, pltpu.roll(value, 1, 1))
-            applied = center * value + turned[part]
-            applied = applied - face_yp * right - face_ym * left
-            applied = applied - face_zp * field[level + 2, part] - face_zm * field[level, part]
-            given = forcing[level, part]
-            rest = given - applied
-            work[level, part] = rest
-            squares[0] = squares[0] + given * given
-            squares[1] = squares[1] + rest * rest
-        return tuple(squares)
-
-    for part in range(2):
-        field[0, part] = none
-        field[length_z + 1, part] = none
-    sine_rows(lambda first: forcing[pl.ds(first, step)], put_work)
-    sweep()
-    sine_rows(lambda first: work[pl.ds(first, step)], put_field)
-    squares = lax.fori_loop(0, length_z, residual, (none, none))
+    def residual(chunk):
+        def run(index, carry):
+            level = first_level + index
+            here = cond[level + 1]
+            right = jnp.where(row_lane == last, here, pltpu.roll(here, last, 1))
+            left = jnp.where(row_lane == 0, here, pltpu.roll(here, 1, 1))
+            face_yp = (0.5 * (here + right))[0:1]
+            face_ym = (0.5 * (here + left))[0:1]
+            face_zp = (0.5 * (here + cond[level + 2]))[0:1]
+            face_zm = (0.5 * (here + cond[level]))[0:1]
+            center = here[0:1] * mode_eig[chunk] + (face_yp + face_ym + face_zp + face_zm)
+            center = center + shift_re
+            values = pair(field, chunk, index + 1)
+            turned = (-shift_im * values[1], shift_im * values[0])
+            above = pair(field, chunk, index + 2)
+            below = pair(field, chunk, index)
+            for part in range(2):
+                value = values[part]
+                right = jnp.where(lane == last, 0.0, pltpu.roll(value, last, 1))
+                left = jnp.where(lane == 0, 0.0, pltpu.roll(value, 1, 1))
+                applied = center * value + turned[part]
+                applied = applied - face_yp * right - face_ym * left
+                applied = applied - face_zp * above[part] - face_zm * below[part]
+                given = forcing[chunk, index, part]
+                rest = given - applied
+                work[chunk, index, part] = rest
+                squares[0] = squares[0] + given * given
+                squares[1] = squares[1] + rest * rest
+            return carry
+
+        lax.fori_loop(0, depth, run, 0)
+
+    squares[0] = none
+    squares[1] = none
+
+    def step(index, carry):
+        @pl.when(index < chunks)
+        def _():
+            chunk = index
+            factors(chunk)
+            for offset in range(1, RADIX):
+                in_copy(chunk, offset).wait()
+            work[chunk, pl.ds(0, depth)] = sine_rows(forcing[chunk])
+            launch(0, chunk)
+
+        @pl.when((index >= 1) & (index < chunks + 1))
+        def _():
+            chunk = index - 1
+            relay(0, chunk)
+            solve(0, chunk)
+            values = sine_rows(work[chunk]) * scale
+            field[chunk, pl.ds(1, depth)] = values[:depth]
+            field[chunk, 0] = values[depth]
+            field[chunk, depth + 1] = values[depth + 1]
+            residual(chunk)
+            work[chunk, pl.ds(0, depth)] = sine_rows(work[chunk, pl.ds(0, depth)])
+            launch(1, chunk)
+
+        @pl.when(index >= 2)
+        def _():
+            chunk = index - 2
+            relay(1, chunk)
+            solve(1, chunk)
+            values = sine_rows(work[chunk, pl.ds(0, depth)]) * scale
+            result[chunk] = field[chunk, pl.ds(1, depth)] + values
+            for offset in (2, 3, 1):
+                out_copy(chunk, offset).start()
+            slabs[side, chunk] = result[chunk, rows(side)]
+
+        return carry
+
+    lax.fori_loop(0, chunks + 2, step, 0)
     row = lax.broadcasted_iota(jnp.int32, (8, 128), 0)
     sums[me] = jnp.where(row == 0, jnp.sum(squares[0]), jnp.sum(squares[1])) / length_x
 
@@ -469,26 +645,20 @@
     def _(offset):
         sum_copy(offset).start()
 
-    sine_rows(lambda first: work[pl.ds(first, step)], put_work)
-    sweep()
-
-    def finish_rows(index, carry):
-        first = index * step
-        values = work[pl.ds(first, step)].reshape(step * 2 * modes, length_y)
-        result = dot3(split(values), sine).reshape(step, 2, modes, length_y)
-        work[pl.ds(first, step)] = field[pl.ds(first + 1, step)] + scale * result
-        for block in range(step // planes):
-            target = index * (step // planes) + block
-            offset = lax.rem(target + groups - me, groups)
-
-            @pl.when(target != me)
+    def settle_sends(index, carry):
+        for turn_id in range(2):
+
+            @pl.when(team < teams - 1)
             def _():
-                out_copy(target, offset).start()
+                up_copy(turn_id, index).wait_send()
+
+            @pl.when(team > 0)
+            def _():
+                down_copy(turn_id, index).wait_send()
 
         return carry
 
-    lax.fori_loop(0, length_z // step, finish_rows, 0)
-    slabs[me] = work[rows(me)]
+    lax.fori_loop(0, chunks, settle_sends, 0)
 
     @each_peer
     def _(offset):
@@ -496,21 +666,22 @@
 
     norms[...] = jnp.sum(sums[...], axis=0)
 
-    @each_peer
-    def _(offset):
-        out_copy(peer(offset), offset).wait()
+    def settle_out(index, carry):
+        for offset in range(1, RADIX):
+            out_copy(index, offset).wait()
+        return carry
+
+    lax.fori_loop(0, chunks, settle_out, 0)
 
     def inverse(plane, carry):
         parts = []
         for residue in range(RADIX):
             blocks = [
-                slabs[residue * owners + owner, plane, part]
-                for part in range(2)
-                for owner in range(owners)
+                slabs[residue, chunk, plane, part] for part in range(2) for chunk in range(chunks)
             ]
             right = split(jnp.concatenate(blocks, axis=0))
-            result = dot3((bwd_hi[residue], bwd_lo[residue]), right)
-            parts.append((result[:count], result[count:]))
+            values = dot3((bwd_hi[residue], bwd_lo[residue]), right)
+            parts.append((values[:count], values[count:]))
         for q in range(RADIX):
             re, im = combine(parts, [residue * q for residue in range(RADIX)])
             out[0, plane, q * count : (q + 1) * count, :] = re
@@ -518,6 +689,9 @@
         return carry
 
     lax.fori_loop(0, planes, inverse, 0)
+
+
+CHUNKS = 4
 
 
 def body(source, layer_ids, conduct_table, shift):
@@ -526,45 +700,61 @@
     length_y = source.shape[3]
     groups = lax.axis_size("gz")
     length_z = planes * groups
-    modes = length_x // groups
-    if groups % RADIX or modes % 8 or length_z % 8 or 8 % planes:
+    count = length_x // RADIX
+    modes = count // CHUNKS
+    if groups % RADIX or groups < 2 * RADIX or modes % 8 or planes > 8 or length_z > 64:
         return body_plain(source, layer_ids, conduct_table, shift)
     me = lax.axis_index("gz")
-    owners = groups // RADIX
+    depth = planes * RADIX
     layers = conduct_table.shape[0]
     onehot = layer_ids[:, :, None] == lax.iota(jnp.int32, layers)[None, None, :]
     conduct = jnp.sum(jnp.where(onehot, conduct_table[None, None, :], 0.0), axis=-1)
     conduct = jnp.pad(conduct, ((0, 8 - planes), (0, 0)))
-    mode_ids = RADIX * (me % owners * modes + lax.iota(jnp.int32, modes)) + me // owners
+    mode_ids = RADIX * lax.iota(jnp.int32, count) + me % RADIX
     mode_eig = 2.0 - 2.0 * jnp.cos(2.0 * jnp.pi / length_x * mode_ids.astype(jnp.float32))
-    mode_eig = jnp.broadcast_to(mode_eig[:, None], (modes, length_y))
+    mode_eig = jnp.broadcast_to(mode_eig[:, None], (count, length_y))
     base = mode_eig + (sine_eigen(length_y) + 2.0)[None, :]
+    mode_eig = mode_eig.reshape(CHUNKS, modes, length_y)
+    base = base.reshape(CHUNKS, modes, length_y)
     forward, backward = radix_tables(length_x)
     tables = [*halves(forward), *halves(backward), *halves(sine_host(length_y))]
-    block = (length_z, 2, modes, length_y)
+    tile = (2, modes, length_y)
     vmem = pl.BlockSpec(memory_space=pltpu.VMEM)
+    hbm = pl.BlockSpec(memory_space=pl.ANY)
+    f32 = jnp.float32
     result, norms = pl.pallas_call(
-        functools.partial(kernel, groups, planes),
+        functools.partial(kernel, groups, planes, CHUNKS),
         out_shape=(
-            jax.ShapeDtypeStruct(source.shape, jnp.float32),
-            jax.ShapeDtypeStruct((8, 128), jnp.float32),
+            jax.ShapeDtypeStruct(source.shape, f32),
+            jax.ShapeDtypeStruct((8, 128), f32),
         ),
-        in_specs=[vmem] * 4 + [pl.BlockSpec(memory_space=pltpu.SMEM)] + [vmem] * 6,
+        in_specs=[hbm] + [vmem] * 3 + [pl.BlockSpec(memory_space=pltpu.SMEM)] + [hbm] * 6,
         out_specs=(vmem, vmem),
-        scratch_shapes=[
-            pltpu.VMEM((groups, planes, 2, modes, length_y), jnp.float32),
-            pltpu.VMEM(block, jnp.float32),
-            pltpu.VMEM((groups, 8, length_y), jnp.float32),
-            pltpu.VMEM((length_z + 2, 8, length_y), jnp.float32),
-            pltpu.VMEM(block, jnp.float32),
-            pltpu.VMEM(block, jnp.float32),
-            pltpu.VMEM((length_z + 2, 2, modes, length_y), jnp.float32),
-            pltpu.VMEM((groups, planes, 2, modes, length_y), jnp.float32),
-            pltpu.VMEM((groups, 8, 128), jnp.float32),
+        scratch_shapes=[pltpu.VMEM(source.shape, f32)]
+        + [pltpu.VMEM(table.shape, jnp.bfloat16) for table in tables]
+        + [
+            pltpu.VMEM((RADIX, CHUNKS, planes, *tile), f32),
+            pltpu.VMEM((CHUNKS, depth, *tile), f32),
+            pltpu.VMEM((groups, 8, length_y), f32),
+            pltpu.VMEM((length_z + 2, 8, length_y), f32),
+            pltpu.VMEM((CHUNKS, depth + 2, *tile), f32),
+            pltpu.VMEM((CHUNKS, length_z + 1, *tile), f32),
+            pltpu.VMEM((CHUNKS, 2, *tile), f32),
+            pltpu.VMEM((CHUNKS, depth + 2, *tile), f32),
+            pltpu.VMEM((CHUNKS, depth, *tile), f32),
+            pltpu.VMEM((RADIX, CHUNKS, planes, *tile), f32),
+            pltpu.VMEM((groups, 8, 128), f32),
+            pltpu.VMEM(tile, f32),
         ]
-        + [pltpu.SemaphoreType.DMA((groups,))] * 8,
+        + [pltpu.VMEM((ITERS, CHUNKS, *tile), f32)] * 4
+        + [pltpu.SemaphoreType.DMA((7,))]
+        + [pltpu.SemaphoreType.DMA((CHUNKS, RADIX))] * 2
+        + [pltpu.SemaphoreType.DMA((groups,))] * 2
+        + [pltpu.SemaphoreType.DMA((CHUNKS, RADIX))] * 2
+        + [pltpu.SemaphoreType.DMA((groups,))] * 2
+        + [pltpu.SemaphoreType.DMA((ITERS, CHUNKS))] * 4,
         compiler_params=pltpu.CompilerParams(
-            collective_id=0, has_side_effects=True, vmem_limit_bytes=48 << 20
+            collective_id=0, has_side_effects=True, vmem_limit_bytes=56 << 20
         ),
     )(source, conduct, mode_eig, base, shift, *tables)
     cells = length_x * length_y * length_z

time: 127 us -> 116 us (0.913)
  the two profiles are of different devices: /device:TPU:27 before, /device:TPU:0 now
where the time goes in v1:
time: 116 us; the launch traced here: 115 us
  Pallas kernels  108 us (93%)
  local copies, waits for them, and re-layouts  4.38 us (4%)
  other arithmetic  2.94 us (3%)
    pallas_call x1, Pallas kernels, body(): pl.pallas_call(functools.partial(kernel, groups, planes, CHUNKS), out_sha...  108 us
    unnamed x1, local copies, waits for them, and re-layouts  3.04 us

profile of v1, /device:TPU:0, one launch (start us, length us, event | category | flops | bytes accessed | tf_op | source)
XLA Modules:
  0.0 115.5 jit_solution(12423542670797995520)
XLA Ops:
  0.7 0.8 select_reduce_fusion
  1.5 0.6 pad.4.conduct
  2.1 0.7 broadcast_add_fusion.base
  2.9 0.7 broadcast_in_dim.24.mode_eig
  3.6 107.5 %shard_map.113 = (f32[2,2,512,256]{3,2,1,0:T(8,128)}, f32[8,128]{1,0:T(8,128)}) custom-call(f32[2,2,512,256]{3,2,1,0:T(8,128)} %source_hbm.1, f32[8,256]{1,0:T(8,128)} %pad.4.conduct, f32[4,32,256]{2,1,0:T(8,128)} %broadcast_in_dim.24.mode_eig, f32[4,32,256]{2,1,0:T(8,128)} %broadcast_add_fusion.base, f32[2]{0:T(128)} %shift.1, ...), custom_call_target="tpu_custom_call" | custom-call | tf_op jit(solution)/shard_map/pallas_call | solution.py:725
  111.1 1.3 %sqrt_reduce_fusion = f32[2]{0:T(128)} fusion(f32[8,128]{1,0:T(8,128)} %get-tuple-element.5), kind=kLoop, calls=%fused_computation.4 | loop fusion | flops 2 | bytes 16 | tf_op jit(solution)/shard_map/sqrt | solution.py:761
  112.4 3.0 %copy.13 = f32[2,2,512,256]{3,2,1,0:T(8,128)} copy(f32[2,2,512,256]{3,2,1,0:T(8,128)} %get-tuple-element.8) | data formatting | bytes 4194304
  (2 shorter events, 0.1 us)

commit v2 on v1

--- a/solution.py
+++ b/solution.py
@@ -350,23 +350,30 @@
             team * RADIX + target,
         )
 
-    def up_copy(turn_id, chunk):
+    def up_copy(turn_id, chunk, source_team, target_team):
         return remote(
             up_out.at[turn_id, chunk],
-            up_in.at[turn_id, chunk],
-            up_send.at[turn_id, chunk],
-            up_recv.at[turn_id, chunk],
-            lax.rem(me + RADIX, groups),
-        )
-
-    def down_copy(turn_id, chunk):
+            up_in.at[turn_id, chunk, source_team],
+            up_send.at[turn_id, chunk, target_team],
+            up_recv.at[turn_id, chunk, source_team],
+            target_team * RADIX + side,
+        )
+
+    def down_copy(turn_id, chunk, source_team, target_team):
         return remote(
             down_out.at[turn_id, chunk],
-            down_in.at[turn_id, chunk],
-            down_send.at[turn_id, chunk],
-            down_recv.at[turn_id, chunk],
-            lax.rem(me + groups - RADIX, groups),
-        )
+            down_in.at[turn_id, chunk, source_team],
+            down_send.at[turn_id, chunk, target_team],
+            down_recv.at[turn_id, chunk, source_team],
+            target_team * RADIX + side,
+        )
+
+    def loop(first, stop, act):
+        def run(index, carry):
+            act(index)
+            return carry
+
+        lax.fori_loop(first, stop, run, 0)
 
     def each_peer(act):
         def run(offset, carry):
@@ -465,8 +472,17 @@
             put(alpha, now, chunk, level)
             return now
 
+        def segment(index, carry):
+            def inner(level, state):
+                now = factor(index * depth + level + 1, state[:2])
+                return (*now, *times(now, state[2:]))
+
+            state = lax.fori_loop(0, depth, inner, (*carry, one, none))
+            put(lines, state[2:], chunk, index)
+            return state[:2]
+
         put(alpha, (none, none), chunk, 0)
-        lax.fori_loop(1, length_z + 1, factor, (none, none))
+        lax.fori_loop(0, teams, segment, (none, none))
 
     sine = (sine_hi[...], sine_lo[...])
 
@@ -474,66 +490,34 @@
         flat = values.reshape(values.shape[0] * 2 * modes, length_y)
         return dot3(split(flat), sine).reshape(values.shape)
 
-    def partial_up(chunk):
-        def run(index, carry):
+    def launch(turn_id, chunk):
+        def rise(index, carry):
             factor = pair(alpha, chunk, first_level + index + 1)
-            value = times(factor, plus(pair(work, chunk, index), carry[:2]))
-            return (*value, *times(factor, carry[2:]))
-
-        return lax.fori_loop(0, depth, run, (none, none, one, none))
-
-    def partial_down(chunk):
-        def run(index, carry):
+            return times(factor, plus(pair(work, chunk, index), carry))
+
+        put(up_out, lax.fori_loop(0, depth, rise, (none, none)), turn_id, chunk)
+        loop(team + 1, teams, lambda target: up_copy(turn_id, chunk, team, target).start())
+
+        def fall(index, carry):
             factor = pair(alpha, chunk, last_level + index + 1)
-            value = times(factor, plus(pair(work, chunk, depth - 1 - index), carry[:2]))
-            return (*value, *times(factor, carry[2:]))
-
-        return lax.fori_loop(0, depth, run, (none, none, one, none))
-
-    def launch(turn_id, chunk):
-        rise = partial_up(chunk)
-        put(up_out, rise[:2], turn_id, chunk)
-
-        @pl.when(team == 0)
-        def _():
-            put(up_in, (none, none), turn_id, chunk)
-            up_copy(turn_id, chunk).start()
-
-        fall = partial_down(chunk)
-        put(down_out, fall[:2], turn_id, chunk)
-
-        @pl.when(team == teams - 1)
-        def _():
-            put(down_in, (none, none), turn_id, chunk)
-            down_copy(turn_id, chunk).start()
-
-        put(lines, rise[2:], chunk, 0)
-        put(lines, fall[2:], chunk, 1)
-
-    def relay(turn_id, chunk):
-        @pl.when(team > 0)
-        def _():
-            up_copy(turn_id, chunk).wait_recv()
-
-            @pl.when(team < teams - 1)
-            def _():
-                more = times(pair(lines, chunk, 0), pair(up_in, turn_id, chunk))
-                put(up_out, plus(pair(up_out, turn_id, chunk), more), turn_id, chunk)
-                up_copy(turn_id, chunk).start()
-
-        @pl.when(team < teams - 1)
-        def _():
-            down_copy(turn_id, chunk).wait_recv()
-
-            @pl.when(team > 0)
-            def _():
-                more = times(pair(lines, chunk, 1), pair(down_in, turn_id, chunk))
-                put(down_out, plus(pair(down_out, turn_id, chunk), more), turn_id, chunk)
-                down_copy(turn_id, chunk).start()
+            return times(factor, plus(pair(work, chunk, depth - 1 - index), carry))
+
+        put(down_out, lax.fori_loop(0, depth, fall, (none, none)), turn_id, chunk)
+        loop(0, team, lambda target: down_copy(turn_id, chunk, team, target).start())
 
     def solve(turn_id, chunk):
-        below = pair(up_in, turn_id, chunk)
-        above = pair(down_in, turn_id, chunk)
+        def gather_up(index, carry):
+            up_copy(turn_id, chunk, index, team).wait_recv()
+            return plus(pair(up_in, turn_id, chunk, index), times(pair(lines, chunk, index), carry))
+
+        def gather_down(index, carry):
+            origin = teams - 1 - index
+            down_copy(turn_id, chunk, origin, team).wait_recv()
+            more = times(pair(lines, chunk, index), carry)
+            return plus(pair(down_in, turn_id, chunk, origin), more)
+
+        below = lax.fori_loop(0, team, gather_up, (none, none))
+        above = lax.fori_loop(0, teams - 1 - team, gather_down, (none, none))
 
         def ahead(index, carry):
             factor = pair(alpha, chunk, first_level + index + 1)
@@ -544,11 +528,11 @@
         reached = lax.fori_loop(0, depth, ahead, below)
         factor = pair(alpha, chunk, first_level + depth)
         edge = pair(alpha, chunk, last_level)
-        loop = times(factor, edge)
-        gap_re = 1.0 - loop[0]
-        inverse = 1.0 / (gap_re * gap_re + loop[1] * loop[1])
+        echo = times(factor, edge)
+        gap_re = 1.0 - echo[0]
+        inverse = 1.0 / (gap_re * gap_re + echo[1] * echo[1])
         top = plus(reached, times(factor, above))
-        top = times(top, (gap_re * inverse, loop[1] * inverse))
+        top = times(top, (gap_re * inverse, echo[1] * inverse))
         outer = plus(above, times(edge, top))
         put(work, outer, chunk, depth + 1)
 
@@ -614,7 +598,6 @@
         @pl.when((index >= 1) & (index < chunks + 1))
         def _():
             chunk = index - 1
-            relay(0, chunk)
             solve(0, chunk)
             values = sine_rows(work[chunk]) * scale
             field[chunk, pl.ds(1, depth)] = values[:depth]
@@ -627,7 +610,6 @@
         @pl.when(index >= 2)
         def _():
             chunk = index - 2
-            relay(1, chunk)
             solve(1, chunk)
             values = sine_rows(work[chunk, pl.ds(0, depth)]) * scale
             result[chunk] = field[chunk, pl.ds(1, depth)] + values
@@ -647,15 +629,8 @@
 
     def settle_sends(index, carry):
         for turn_id in range(2):
-
-            @pl.when(team < teams - 1)
-            def _():
-                up_copy(turn_id, index).wait_send()
-
-            @pl.when(team > 0)
-            def _():
-                down_copy(turn_id, index).wait_send()
-
+            loop(team + 1, teams, lambda target: up_copy(turn_id, index, team, target).wait_send())
+            loop(0, team, lambda target: down_copy(turn_id, index, team, target).wait_send())
         return carry
 
     lax.fori_loop(0, chunks, settle_sends, 0)
@@ -739,22 +714,26 @@
             pltpu.VMEM((length_z + 2, 8, length_y), f32),
             pltpu.VMEM((CHUNKS, depth + 2, *tile), f32),
             pltpu.VMEM((CHUNKS, length_z + 1, *tile), f32),
-            pltpu.VMEM((CHUNKS, 2, *tile), f32),
+            pltpu.VMEM((CHUNKS, groups // RADIX, *tile), f32),
             pltpu.VMEM((CHUNKS, depth + 2, *tile), f32),
             pltpu.VMEM((CHUNKS, depth, *tile), f32),
             pltpu.VMEM((RADIX, CHUNKS, planes, *tile), f32),
             pltpu.VMEM((groups, 8, 128), f32),
             pltpu.VMEM(tile, f32),
         ]
-        + [pltpu.VMEM((ITERS, CHUNKS, *tile), f32)] * 4
+        + [
+            pltpu.VMEM((ITERS, CHUNKS, *tile), f32),
+            pltpu.VMEM((ITERS, CHUNKS, groups // RADIX, *tile), f32),
+        ]
+        * 2
         + [pltpu.SemaphoreType.DMA((7,))]
         + [pltpu.SemaphoreType.DMA((CHUNKS, RADIX))] * 2
         + [pltpu.SemaphoreType.DMA((groups,))] * 2
         + [pltpu.SemaphoreType.DMA((CHUNKS, RADIX))] * 2
         + [pltpu.SemaphoreType.DMA((groups,))] * 2
-        + [pltpu.SemaphoreType.DMA((ITERS, CHUNKS))] * 4,
+        + [pltpu.SemaphoreType.DMA((ITERS, CHUNKS, groups // RADIX))] * 4,
         compiler_params=pltpu.CompilerParams(
-            collective_id=0, has_side_effects=True, vmem_limit_bytes=56 << 20
+            collective_id=0, has_side_effects=True, vmem_limit_bytes=44 << 20
         ),
     )(source, conduct, mode_eig, base, shift, *tables)
     cells = length_x * length_y * length_z

time: 116 us -> 88.5 us (0.76)
  Pallas kernels: 108 us -> 76.2 us
  local copies, waits for them, and re-layouts: 4.38 us -> 9.62 us
  other arithmetic: 2.94 us -> 1.6 us
    pallas_call x1, Pallas kernels: 108 us -> 76.2 us  [body(): pl.pallas_call(functools.partial(kernel, groups, planes, CHUNKS), out_sha...]
    unnamed x1 -> x17, local copies, waits for them, and re-layouts: 3.04 us -> 9.53 us
where the time goes in v2:
time: 88.5 us; the launch traced here: 88.1 us
  Pallas kernels  76.2 us (86%)
  local copies, waits for them, and re-layouts  9.62 us (11%)
  other arithmetic  1.6 us (2%)
    pallas_call x1, Pallas kernels, body(): pl.pallas_call(functools.partial(kernel, groups, planes, CHUNKS), out_sha...  76.2 us
    unnamed x17, local copies, waits for them, and re-layouts  9.53 us

profile of v2, /device:TPU:0, one launch (start us, length us, event | category | flops | bytes accessed | tf_op | source)
XLA Modules:
  0.0 88.1 jit_solution(4471503081058140690)
XLA Ops:
  0.7 0.8 select_reduce_fusion
  1.5 0.1 broadcast_add_fusion.base
  1.6 0.1 broadcast_in_dim.24.mode_eig
  1.7 0.0 copy-start
  1.7 1.6 %copy-done = f32[2,2,512,256]{3,2,1,0:T(8,128)S(1)} copy-done((f32[2,2,512,256]{3,2,1,0:T(8,128)S(1)}, f32[2,2,512,256]{3,2,1,0:T(8,128)}, u32[]{:S(2)}) %copy-start) | copy-done | bytes 2097176
  3.3 0.0 copy-start.1
  3.3 1.0 %copy-done.1 = bf16[4,256,256]{2,1,0:T(8,128)(2,1)S(1)} copy-done((bf16[4,256,256]{2,1,0:T(8,128)(2,1)S(1)}, bf16[4,256,256]{2,1,0:T(8,128)(2,1)}, u32[]{:S(2)}) %copy-start.1) | copy-done | bytes 524312
  4.3 0.0 copy-start.2
  4.4 1.0 %copy-done.2 = bf16[4,256,256]{2,1,0:T(8,128)(2,1)S(1)} copy-done((bf16[4,256,256]{2,1,0:T(8,128)(2,1)S(1)}, bf16[4,256,256]{2,1,0:T(8,128)(2,1)}, u32[]{:S(2)}) %copy-start.2) | copy-done | bytes 524312
  5.4 0.0 copy-start.3
  5.4 1.0 %copy-done.3 = bf16[4,256,256]{2,1,0:T(8,128)(2,1)S(1)} copy-done((bf16[4,256,256]{2,1,0:T(8,128)(2,1)S(1)}, bf16[4,256,256]{2,1,0:T(8,128)(2,1)}, u32[]{:S(2)}) %copy-start.3) | copy-done | bytes 524312
  6.4 0.0 copy-start.4
  6.4 1.0 %copy-done.4 = bf16[4,256,256]{2,1,0:T(8,128)(2,1)S(1)} copy-done((bf16[4,256,256]{2,1,0:T(8,128)(2,1)S(1)}, bf16[4,256,256]{2,1,0:T(8,128)(2,1)}, u32[]{:S(2)}) %copy-start.4) | copy-done | bytes 524312
  7.5 0.0 copy-start.5
  7.5 0.9 %copy-done.5 = bf16[256,256]{1,0:T(8,128)(2,1)S(1)} copy-done((bf16[256,256]{1,0:T(8,128)(2,1)S(1)}, bf16[256,256]{1,0:T(8,128)(2,1)}, u32[]{:S(2)}) %copy-start.5) | copy-done | bytes 131096
  8.4 0.0 copy-start.6
  8.4 0.9 %copy-done.6 = bf16[256,256]{1,0:T(8,128)(2,1)S(1)} copy-done((bf16[256,256]{1,0:T(8,128)(2,1)S(1)}, bf16[256,256]{1,0:T(8,128)(2,1)}, u32[]{:S(2)}) %copy-start.6) | copy-done | bytes 131096
  9.3 0.0 copy-start.7
  9.3 0.7 copy-done.7
  9.9 76.2 %shard_map.113 = (f32[2,2,512,256]{3,2,1,0:T(8,128)S(1)}, f32[8,128]{1,0:T(8,128)S(1)}) custom-call(f32[2,2,512,256]{3,2,1,0:T(8,128)S(1)} %copy-done, f32[8,256]{1,0:T(8,128)S(1)} %pad.4.conduct, f32[4,32,256]{2,1,0:T(8,128)S(1)} %broadcast_in_dim.24.mode_eig, f32[4,32,256]{2,1,0:T(8,128)S(1)} %broadcast_add_fusion.base, f32[2]{0:T(128)S(1)} %copy-done.7, ...), custom_call_target="tpu_custom_call" | custom-call | tf_op jit(solution)/shard_map/pallas_call | solution.py:700
  86.2 0.6 sqrt_reduce_fusion
  86.8 1.3 %copy.13 = f32[2,2,512,256]{3,2,1,0:T(8,128)} copy(f32[2,2,512,256]{3,2,1,0:T(8,128)S(1)} %get-tuple-element.8) | data formatting | bytes 4194304
  (3 shorter events, 0.1 us)
Async XLA Ops:
  1.7 1.6 %copy-start = (f32[2,2,512,256]{3,2,1,0:T(8,128)S(1)}, f32[2,2,512,256]{3,2,1,0:T(8,128)}, u32[]{:S(2)}) copy-start(f32[2,2,512,256]{3,2,1,0:T(8,128)} %source_hbm.1) | copy-start | bytes 6291460
  3.3 1.0 %copy-start.1 = (bf16[4,256,256]{2,1,0:T(8,128)(2,1)S(1)}, bf16[4,256,256]{2,1,0:T(8,128)(2,1)}, u32[]{:S(2)}) copy-start(bf16[4,256,256]{2,1,0:T(8,128)(2,1)} %constant.53.clone.bwd_lo_hbm) | copy-start | bytes 1572868
  4.3 1.0 %copy-start.2 = (bf16[4,256,256]{2,1,0:T(8,128)(2,1)S(1)}, bf16[4,256,256]{2,1,0:T(8,128)(2,1)}, u32[]{:S(2)}) copy-start(bf16[4,256,256]{2,1,0:T(8,128)(2,1)} %constant.52.clone.bwd_hi_hbm) | copy-start | bytes 1572868
  5.4 1.0 %copy-start.3 = (bf16[4,256,256]{2,1,0:T(8,128)(2,1)S(1)}, bf16[4,256,256]{2,1,0:T(8,128)(2,1)}, u32[]{:S(2)}) copy-start(bf16[4,256,256]{2,1,0:T(8,128)(2,1)} %constant.51.clone.fwd_lo_hbm) | copy-start | bytes 1572868
  6.4 1.0 %copy-start.4 = (bf16[4,256,256]{2,1,0:T(8,128)(2,1)S(1)}, bf16[4,256,256]{2,1,0:T(8,128)(2,1)}, u32[]{:S(2)}) copy-start(bf16[4,256,256]{2,1,0:T(8,128)(2,1)} %constant.50.clone.fwd_hi_hbm) | copy-start | bytes 1572868
  7.5 0.9 %copy-start.5 = (bf16[256,256]{1,0:T(8,128)(2,1)S(1)}, bf16[256,256]{1,0:T(8,128)(2,1)}, u32[]{:S(2)}) copy-start(bf16[256,256]{1,0:T(8,128)(2,1)} %constant.55.clone.sine_lo_hbm) | copy-start | bytes 393220
  8.4 0.9 %copy-start.6 = (bf16[256,256]{1,0:T(8,128)(2,1)S(1)}, bf16[256,256]{1,0:T(8,128)(2,1)}, u32[]{:S(2)}) copy-start(bf16[256,256]{1,0:T(8,128)(2,1)} %constant.54.clone.sine_hi_hbm) | copy-start | bytes 393220
  9.3 0.7 copy-start.7

commit v3 on v2

--- a/solution.py
+++ b/solution.py
@@ -733,7 +733,7 @@
         + [pltpu.SemaphoreType.DMA((groups,))] * 2
         + [pltpu.SemaphoreType.DMA((ITERS, CHUNKS, groups // RADIX))] * 4,
         compiler_params=pltpu.CompilerParams(
-            collective_id=0, has_side_effects=True, vmem_limit_bytes=44 << 20
+            collective_id=0, has_side_effects=True, vmem_limit_bytes=58 << 20
         ),
     )(source, conduct, mode_eig, base, shift, *tables)
     cells = length_x * length_y * length_z

time: 88.5 us -> 85.6 us (0.967)
  local copies, waits for them, and re-layouts: 9.62 us -> 4.38 us
  other arithmetic: 1.6 us -> 2.94 us
  Pallas kernels: 76.2 us -> 77.4 us
    unnamed x17 -> x1, local copies, waits for them, and re-layouts: 9.53 us -> 3.04 us
    pallas_call x1, Pallas kernels: 76.2 us -> 77.4 us  [body(): pl.pallas_call(functools.partial(kernel, groups, planes, CHUNKS), out_sha...]
where the time goes in v3:
time: 85.6 us; the launch traced here: 85.4 us
  Pallas kernels  77.4 us (90%)
  local copies, waits for them, and re-layouts  4.38 us (5%)
  other arithmetic  2.94 us (3%)
    pallas_call x1, Pallas kernels, body(): pl.pallas_call(functools.partial(kernel, groups, planes, CHUNKS), out_sha...  77.4 us
    unnamed x1, local copies, waits for them, and re-layouts  3.04 us

profile of v3, /device:TPU:0, one launch (start us, length us, event | category | flops | bytes accessed | tf_op | source)
XLA Modules:
  0.0 85.4 jit_solution(9699420135006466780)
XLA Ops:
  0.7 0.8 select_reduce_fusion
  1.5 0.6 pad.4.conduct
  2.1 0.7 broadcast_add_fusion.base
  2.9 0.7 broadcast_in_dim.24.mode_eig
  3.6 77.4 %shard_map.113 = (f32[2,2,512,256]{3,2,1,0:T(8,128)}, f32[8,128]{1,0:T(8,128)}) custom-call(f32[2,2,512,256]{3,2,1,0:T(8,128)} %source_hbm.1, f32[8,256]{1,0:T(8,128)} %pad.4.conduct, f32[4,32,256]{2,1,0:T(8,128)} %broadcast_in_dim.24.mode_eig, f32[4,32,256]{2,1,0:T(8,128)} %broadcast_add_fusion.base, f32[2]{0:T(128)} %shift.1, ...), custom_call_target="tpu_custom_call" | custom-call | tf_op jit(solution)/shard_map/pallas_call | solution.py:700
  81.0 1.3 %sqrt_reduce_fusion = f32[2]{0:T(128)} fusion(f32[8,128]{1,0:T(8,128)} %get-tuple-element.5), kind=kLoop, calls=%fused_computation.4 | loop fusion | flops 2 | bytes 16 | tf_op jit(solution)/shard_map/sqrt | solution.py:740
  82.3 3.0 %copy.13 = f32[2,2,512,256]{3,2,1,0:T(8,128)} copy(f32[2,2,512,256]{3,2,1,0:T(8,128)} %get-tuple-element.8) | data formatting | bytes 4194304
  (2 shorter events, 0.1 us)
